TPU v7x, 128 devices: a whole 4x4x4 slice. The times are simulated.
128 devices in a mesh: row: 16 (over z, x), col: 8 (over y, core).
Axes of the slice: x: 4, y: 4, z: 4, core: 2. Of those that a mesh axis runs over, the one named last changes fastest.
Arguments:
- edge_vec: float32 [3, 1024], P(None, ('row', 'col')), may hold values from -8 to 8
- edge_atoms: int32 [2, 1024], P(None, ('row', 'col')), may hold values from 0 to 95
- block_weight: bfloat16 [144, 16384], replicated, may hold values from -0.5 to 0.5
- base_hamiltonian: bfloat16 [12288, 12288], P('row', 'col'), as said below
- lower_bound: float32 [1], replicated, may hold values from -50 to -40
- upper_bound: float32 [1], replicated, may hold values from 40 to 50
Outputs:
- purified: float32 [12288, 12288], P('row', 'col')
Inputs may be any that keep to these rules, and one draw needn't show every extreme that they name: `base_hamiltonian`: symmetric.
All inputs are finite; a program needn't handle non-finite values.
Results may differ from a plain program's by a relative error of at most 0.0031.
Values may be sent and summed in bfloat16 or wider, within the bound.
A program may use at most 192 MiB of HBM per device.

v0:
```python
import jax
import jax.numpy as jnp
from jax import lax
from jax.sharding import PartitionSpec as P

ORB = 128
NR = 16
RB = 6


def features(edge_vec):
    squared = jnp.sum(edge_vec * edge_vec, axis=0)
    radius = jnp.sqrt(squared + 0.25)
    unit_x = edge_vec[0] / radius
    unit_y = edge_vec[1] / radius
    unit_z = edge_vec[2] / radius
    harmonics = jnp.stack(
        [
            jnp.ones_like(unit_x),
            unit_x,
            unit_y,
            unit_z,
            unit_x * unit_y,
            unit_y * unit_z,
            unit_z * unit_x,
            unit_x * unit_x - unit_y * unit_y,
            3.0 * unit_z * unit_z - 1.0,
        ]
    )
    centers = 1.0 + 0.3 * jnp.arange(NR, dtype=jnp.float32)
    radial = jnp.exp(-jnp.square((radius[None, :] - centers[:, None]) / 0.5))
    return (radial[:, None, :] * harmonics[None, :, :]).reshape(NR * 9, edge_vec.shape[1])


def shards(edge_vec, edge_atoms, block_weight, base_hamiltonian, lower_bound, upper_bound):
    atoms_float = edge_atoms.astype(jnp.float32)
    packed = jnp.concatenate([features(edge_vec), atoms_float], axis=0)
    gathered = lax.all_gather(packed, ("row", "col"), axis=1, tiled=True)
    embedding = gathered[:-2]
    atom_pairs = gathered[-2:].astype(jnp.int32)
    first_atom = atom_pairs[0]
    second_atom = atom_pairs[1]
    atoms_total = RB * lax.axis_size("row")
    col_blocks = atoms_total // lax.axis_size("col")
    row_index = lax.axis_index("row")
    col_index = lax.axis_index("col")
    row_atoms = row_index * RB + jnp.arange(RB, dtype=jnp.int32)
    col_atoms = col_index * col_blocks + jnp.arange(col_blocks, dtype=jnp.int32)
    direct = (
        (
            (first_atom[None, None, :] == row_atoms[:, None, None])
            & (second_atom[None, None, :] == col_atoms[None, :, None])
        )
        .astype(jnp.float32)
        .reshape(RB * col_blocks, -1)
    )
    mirror = (
        (
            (first_atom[None, None, :] == col_atoms[None, :, None])
            & (second_atom[None, None, :] == row_atoms[:, None, None])
        )
        .astype(jnp.float32)
        .reshape(RB * col_blocks, -1)
    )
    contract = (((1,), (1,)), ((), ()))
    coefficient = lax.dot_general(
        direct, embedding, contract, precision=lax.Precision.HIGHEST
    ).astype(jnp.bfloat16)
    coefficient_back = lax.dot_general(
        mirror, embedding, contract, precision=lax.Precision.HIGHEST
    ).astype(jnp.bfloat16)
    blocks = jnp.dot(coefficient, block_weight, preferred_element_type=jnp.float32).reshape(
        RB, col_blocks, ORB, ORB
    )
    blocks_back = jnp.dot(
        coefficient_back, block_weight, preferred_element_type=jnp.float32
    ).reshape(RB, col_blocks, ORB, ORB)
    tile_rows = RB * ORB
    tile_cols = col_blocks * ORB
    hamiltonian = (
        (blocks + blocks_back.transpose(0, 1, 3, 2))
        .transpose(0, 2, 1, 3)
        .reshape(tile_rows, tile_cols)
    )
    hamiltonian = hamiltonian + base_hamiltonian.astype(jnp.float32)
    global_rows = row_index * tile_rows + jnp.arange(tile_rows, dtype=jnp.int32)
    global_cols = col_index * tile_cols + jnp.arange(tile_cols, dtype=jnp.int32)
    diagonal_mask = global_rows[:, None] == global_cols[None, :]
    shifted = jnp.where(diagonal_mask, upper_bound[0], jnp.float32(0.0)) - hamiltonian
    start_density = (shifted / (upper_bound[0] - lower_bound[0])).astype(jnp.bfloat16)
    row_strip = lax.all_gather(start_density, "col", axis=1, tiled=True)
    return jnp.dot(
        row_strip,
        lax.all_gather(start_density, "row", axis=0, tiled=True),
        preferred_element_type=jnp.float32,
    )


def solution(mesh):
    return jax.shard_map(
        shards,
        mesh=mesh,
        in_specs=(P(None, ("row", "col")), P(None, ("row", "col")), P(), P("row", "col"), P(), P()),
        out_specs=P("row", "col"),
        check_vma=False,
    )
```

profile of v0, /device:TPU:1, one launch (start us, length us, event | category | flops | bytes accessed | tf_op | source)
XLA Modules:
  0.0 437.2 jit_solution(4057055565434168536)
XLA Ops:
  6.5 0.7 multiply_reduce_fusion
  7.3 0.8 multiply_subtract_fusion
  9.4 0.8 fusion.6
  10.2 0.1 copy.13
  10.3 0.8 copy.14
  11.1 0.1 negate_exponential_fusion
  11.2 0.1 broadcast_multiply_fusion
  11.3 0.1 mul.81
  11.3 0.1 pad_maximum_fusion
  11.4 39.7 %all_gather.9 = f32[146,1024]{0,1:T(8,128)S(1)} all-gather(f32[146,8]{0,1:T(8,128)S(1)} %pad_maximum_fusion), channel_id=1, replica_groups=mesh['row'=16,'col'=8] {'row','col'}, dimensions={1}, use_global_device_ids=true | all-gather | bytes 602688 | tf_op jit(solution)/shard_map/all_gather | solution.py:38
  51.1 0.2 slice_convert_fusion
  51.3 0.5 slice_reduce_fusion.1
  51.8 0.1 broadcast_compare_fusion.3
  51.9 0.1 broadcast_compare_fusion.1
  52.0 0.1 broadcast_and_fusion
  52.1 0.5 convolution_convert_fusion
  52.7 0.0 slice-start
  52.7 0.5 convolution_convert_fusion.1
  53.2 0.0 slice-start.1
  53.3 3.4 convolution_bitcast_fusion.1
  56.6 3.1 copy.17
  59.7 0.8 convolution_bitcast_fusion
  60.5 3.0 copy.18
  63.5 6.6 %copy.15 = f32[6,12,128,128]{2,1,3,0:T(8,128)} copy(f32[6,12,128,128]{3,2,1,0:T(8,128)} %bitcast.52) | data formatting | bytes 9437184 | tf_op jit(solution)/shard_map/reshape | solution.py:77
  70.1 7.3 %bitcast_add_fusion = f32[6,12,128,128]{3,1,2,0:T(8,128)S(1)} fusion(f32[6,12,128,128]{2,1,3,0:T(8,128)} %copy.15, f32[6,12,128,128]{3,2,1,0:T(8,128)} %bitcast.51), kind=kLoop, calls=%fused_computation | loop fusion | flops 1179648 | bytes 14155776 | tf_op jit(solution)/shard_map/add | solution.py:81
  77.3 4.2 fusion.2
  81.6 0.0 all-gather.3.cloned.1.call-update
  81.6 0.0 all-gather.5.cloned.1.call-start
  81.6 0.7 all-gather.5.cloned.1.call-update
  82.3 91.0 %all-gather.3.cloned.1.call-done = bf16[768,12288]{1,0:T(8,128)(2,1)} async-done(((bf16[768,1536]{1,0:T(8,128)(2,1)}), bf16[768,12288]{1,0:T(8,128)(2,1)}) %all-gather.3.cloned.1.call-update) | async-done | bytes 18874384 | tf_op jit(solution)/shard_map/all_gather | solution.py:91
  173.4 220.8 %all-gather.5.cloned.1.call-done = bf16[12288,1536]{1,0:T(8,128)(2,1)} async-done(((bf16[768,1536]{1,0:T(8,128)(2,1)}), bf16[12288,1536]{1,0:T(8,128)(2,1)}) %all-gather.5.cloned.1.call-update) | async-done | bytes 37748752 | tf_op jit(solution)/shard_map/all_gather | solution.py:94
  394.2 36.2 %fusion.8 = f32[768,1536]{1,0:T(8,128)} fusion(bf16[768,12288]{1,0:T(8,128)(2,1)} %all-gather.3.cloned.1.call-done, bf16[12288,1536]{1,0:T(8,128)(2,1)} %all-gather.5.cloned.1.call-done), kind=kOutput, calls=%fused_computation.42 | convolution fusion | flops 28991029248 | bytes 61341696 | tf_op jit(solution)/shard_map/dot_general | solution.py:92
  (18 shorter events, 0.2 us)
Async XLA Ops:
  6.5 166.9 %all-gather.3.cloned.1.call-start = ((), (), s32[]{:S(2)}) async-start(), calls=%async_computation | async-start | bytes 21233664 | tf_op jit(solution)/shard_map/all_gather | solution.py:91
  52.7 7.0 %slice-start = ((s8[4718592]{0:T(1024)(128)(4,1)}), s8[4194304]{0:T(1024)(128)(4,1)S(1)}, s32[]{:S(2)}) async-start(s8[4718592]{0:T(1024)(128)(4,1)} %bitcast.49), calls=%async_computation.2 | async-start | bytes 8388608
  53.2 6.5 %slice-start.1 = ((s8[4718592]{0:T(1024)(128)(4,1)}), s8[524288]{0:T(1024)(128)(4,1)S(1)}, s32[]{:S(2)}) async-start(s8[4718592]{0:T(1024)(128)(4,1)} %bitcast.49), calls=%async_computation.3 | async-start | bytes 1048576
  70.1 7.3 %copy-start = (bf16[768,1536]{1,0:T(8,128)(2,1)S(1)}, bf16[768,1536]{1,0:T(8,128)(2,1)}, u32[]{:S(2)}) copy-start(bf16[768,1536]{1,0:T(8,128)(2,1)} %param.9) | copy-start | bytes 7077892
  81.6 312.6 %all-gather.5.cloned.1.call-start = ((), (), s32[]{:S(2)}) async-start(), calls=%async_computation.1 | async-start | bytes 40108032 | tf_op jit(solution)/shard_map/all_gather | solution.py:94
Sparse Core Ops, SparseCore 0:
  81.7 91.6 all-gather.2
  175.5 218.6 all-gather.4
where the time goes:
time: 438 us; the launch traced here: 437 us
  waiting for transfers between devices  313 us (71%)
  matrix products  41.4 us (9%)
  blocking collectives  39.7 us (9%)
  between operations  14.8 us (3%)
  other arithmetic  14.5 us (3%)
  local copies, waits for them, and re-layouts  14.2 us (3%)
    all_gather x1, waiting for transfers between devices, shards(): lax.all_gather(start_density, 'row', axis=0, tiled=True)  221 us
    all_gather x1, waiting for transfers between devices, shards(): row_strip = lax.all_gather(start_density, 'col', axis=1, tiled=True)  91 us
    all_gather x1, blocking collectives, shards(): gathered = lax.all_gather(packed, ('row', 'col'), axis=1, tiled=True)  39.7 us
    dot_general x1, matrix products, shards(): jnp.dot(row_strip, lax.all_gather(start_density, 'row', axis=0, tiled=Tru...  36.2 us
  transfers between devices with their start and end apart: 2, of which 2 were waited for; matrix products, arithmetic and copies ran while one was open for 0% of the time, Pallas kernels for 0%

commit v1 on v0

--- a/solution.py
+++ b/solution.py
@@ -88,7 +88,8 @@
     diagonal_mask = global_rows[:, None] == global_cols[None, :]
     shifted = jnp.where(diagonal_mask, upper_bound[0], jnp.float32(0.0)) - hamiltonian
     start_density = (shifted / (upper_bound[0] - lower_bound[0])).astype(jnp.bfloat16)
-    row_strip = lax.all_gather(start_density, "col", axis=1, tiled=True)
+    repeated = jnp.stack([start_density] * lax.axis_size("col"))
+    row_strip = jnp.concatenate(lax.all_to_all(repeated, "col", 0, 0), axis=1)
     return jnp.dot(
         row_strip,
         lax.all_gather(start_density, "row", axis=0, tiled=True),

time: 438 us -> 348 us (0.79)
  waiting for transfers between devices: 313 us -> 1.86 us
  blocking collectives: 39.7 us -> 250 us
    all_gather x1, waiting for transfers between devices: 221 us -> 1.85 us  [shards(): lax.all_gather(start_density, 'row', axis=0, tiled=True)]
    all_to_all x0 -> x1, blocking collectives: none -> 210 us  [shards(): row_strip = jnp.concatenate(lax.all_to_all(repeated, 'col', 0, 0), axis=1)]
    all_gather x1 -> x0, waiting for transfers between devices: 91 us -> none  [shards(): row_strip = lax.all_gather(start_density, 'col', axis=1, tiled=True)]
  transfers between devices with their start and end apart: 2 -> 1, of which waited for: 2 -> 1; matrix products, arithmetic and copies ran while one was open for 0% -> 1% of each run, Pallas kernels for 0% -> 0%
where the time goes in v1:
time: 348 us; the launch traced here: 347 us
  blocking collectives  250 us (72%)
  matrix products  43.8 us (13%)
  other arithmetic  18.8 us (5%)
  local copies, waits for them, and re-layouts  18.4 us (5%)
  between operations  14.8 us (4%)
    all_to_all x1, blocking collectives, shards(): row_strip = jnp.concatenate(lax.all_to_all(repeated, 'col', 0, 0), axis=1)  210 us
    all_gather x1, blocking collectives, shards(): gathered = lax.all_gather(packed, ('row', 'col'), axis=1, tiled=True)  39.6 us
    dot_general x1, matrix products, shards(): jnp.dot(row_strip, lax.all_gather(start_density, 'row', axis=0, tiled=Tru...  36.5 us
    add x1, other arithmetic, shards(): blocks + blocks_back.transpose(0, 1, 3, 2)  9.91 us
  transfers between devices with their start and end apart: 1, of which 1 were waited for; matrix products, arithmetic and copies ran while one was open for 1% of the time, Pallas kernels for 0%

profile of v1, /device:TPU:1, one launch (start us, length us, event | category | flops | bytes accessed | tf_op | source)
XLA Modules:
  0.0 347.3 jit_solution(12743069790894474994)
XLA Ops:
  6.5 0.0 all-gather.2.cloned.1.call-start
  6.5 0.7 multiply_reduce_fusion
  7.2 0.8 multiply_subtract_fusion
  8.0 0.8 fusion.6
  8.9 0.1 copy.14
  9.0 0.1 negate_exponential_fusion
  9.1 0.1 broadcast_multiply_fusion
  9.2 0.1 mul.81
  9.2 0.8 copy.15
  10.0 0.1 pad_maximum_fusion
  10.1 39.6 %all_gather.6 = f32[146,1024]{0,1:T(8,128)S(1)} all-gather(f32[146,8]{0,1:T(8,128)S(1)} %pad_maximum_fusion), channel_id=1, replica_groups=mesh['row'=16,'col'=8] {'row','col'}, dimensions={1}, use_global_device_ids=true | all-gather | bytes 602688 | tf_op jit(solution)/shard_map/all_gather | solution.py:38
  49.7 0.2 slice_convert_fusion
  49.9 0.5 slice_reduce_fusion.1
  50.5 0.1 broadcast_compare_fusion.1
  50.6 0.1 broadcast_compare_fusion.3
  50.7 0.1 broadcast_and_fusion
  50.8 0.5 convolution_convert_fusion
  51.3 3.1 convolution_bitcast_fusion
  54.5 3.0 copy.20
  57.5 6.6 %copy.16 = f32[6,12,128,128]{2,1,3,0:T(8,128)} copy(f32[6,12,128,128]{3,2,1,0:T(8,128)} %bitcast.54) | data formatting | bytes 9437184 | tf_op jit(solution)/shard_map/reshape | solution.py:77
  64.1 0.5 convolution_convert_fusion.1
  64.7 3.1 convolution_bitcast_fusion.1
  67.8 3.0 copy.19
  72.1 0.0 copy-start
  72.1 9.9 %bitcast_add_fusion = f32[6,12,128,128]{3,1,2,0:T(8,128)} fusion(f32[6,12,128,128]{2,1,3,0:T(8,128)} %copy.16, f32[6,12,128,128]{3,2,1,0:T(8,128)} %bitcast.53), kind=kLoop, calls=%fused_computation | loop fusion | flops 1179648 | bytes 14155776 | tf_op jit(solution)/shard_map/add | solution.py:81
  82.0 5.9 %fusion.2 = bf16[768,1536]{1,0:T(8,128)(2,1)} fusion(f32[96,8,12,128]{3,2,1,0:T(8,128)} %bitcast.51, bf16[768,1536]{1,0:T(8,128)(2,1)S(1)} %copy-done, f32[]{:T(128)S(6)} %sub.36, f32[]{:T(128)} %bitcast.49, s32[1536]{0:T(1024)S(1)} %iota_add_fusion, s32[768]{0:T(1024)S(1)} %iota_add_fusion.1), kind=kLoop, calls=%fused_computation.4 | loop fusion | flops 8257536 | bytes 9446408 | tf_op jit(solution)/shard_map/convert_element_type | solution.py:90
  87.9 0.0 all-gather.2.cloned.1.call-update
  87.9 2.8 copy.18
  90.7 1.4 stack.5
  92.2 209.9 %all_to_all.5 = bf16[8,768,1536]{1,2,0:T(8,128)(2,1)} all-to-all(bf16[8,768,1536]{1,2,0:T(8,128)(2,1)S(1)} %stack.5), channel_id=1, replica_groups=mesh['row'=16,'col'=8] {'col'}, dimensions={0} | all-to-all | bytes 37748736 | tf_op jit(solution)/shard_map/all_to_all | solution.py:92
  302.1 1.8 all-gather.2.cloned.1.call-done
  303.9 36.5 %fusion.8 = f32[768,1536]{1,0:T(8,128)} fusion(bf16[768,12288]{0,1:T(8,128)(2,1)} %bitcast.52, bf16[12288,1536]{1,0:T(8,128)(2,1)} %all-gather.2.cloned.1.call-done), kind=kOutput, calls=%fused_computation.42 | convolution fusion | flops 28991029248 | bytes 61341696 | tf_op jit(solution)/shard_map/dot_general | solution.py:93
  (13 shorter events, 0.2 us)
Async XLA Ops:
  6.5 297.4 %all-gather.2.cloned.1.call-start = ((), (), s32[]{:S(2)}) async-start(), calls=%async_computation.1 | async-start | bytes 40108032 | tf_op jit(solution)/shard_map/all_gather | solution.py:95
  72.1 9.9 %copy-start = (bf16[768,1536]{1,0:T(8,128)(2,1)S(1)}, bf16[768,1536]{1,0:T(8,128)(2,1)}, u32[]{:S(2)}) copy-start(bf16[768,1536]{1,0:T(8,128)(2,1)} %param.9) | copy-start | bytes 7077892
Sparse Core Ops, SparseCore 0:
  88.0 215.8 all-gather.1
